TPU v7x, 32 devices: a whole 2x2x4 slice. The times are simulated.
32 devices in a mesh: tok: 16 (over z, x, core), col: 2 (over y).
Axes of the slice: x: 2, y: 2, z: 4, core: 2. Of those that a mesh axis runs over, the one named last changes fastest.
Arguments:
- tokens: bfloat16 [12288, 2048], P('tok', 'col'), may hold values from -6 to 6
- cotangent: bfloat16 [12288, 2048], P('tok', 'col'), may hold values from -6 to 6
- query_weight: bfloat16 [2048, 2048], P(None, 'col'), may hold values from -1 to 1
- slot_keys: bfloat16 [16384, 2048], P('tok', 'col'), may hold values from -64 to 64
- values: float32 [16384, 2048], P('tok', 'col'), may hold values from -6 to 6
- momentum: float32 [16384, 2048], P('tok', 'col'), may hold values from -0.3 to 0.3
- page_ids: int32 [192, 4], P('tok'), may hold values from 0 to 127, as said below
- last_step: int32 [128], P('tok'), may hold values from 0 to 63
- decay_rate: float32 [2048], P('col'), may hold values from 0.004 to 0.08
- gate_weight: bfloat16 [2048, 2048], P(None, 'col'), may hold values from -0.125 to 0.125
- out_weight: bfloat16 [2048, 2048], P('col'), may hold values from -0.1875 to 0.1875
Outputs:
- layer_out: bfloat16 [12288, 2048], P('tok', 'col')
- new_values: float32 [16384, 2048], P('tok', 'col')
- new_momentum: float32 [16384, 2048], P('tok', 'col')
Inputs may be any that keep to these rules, and one draw needn't show every extreme that they name: `page_ids`: page p belongs to owner group p // 8. Among the 48 pages listed by the blocks of one index of tok, counted with repeats, at most 4 belong to any one owner group, and one owner group gets exactly 4 from every index of tok. A block may list a page more than once.
All inputs are finite; a program needn't handle non-finite values.
Results may differ from a plain program's by a relative error of at most 0.014.
Values may be sent and summed in bfloat16 or wider, within the bound.
No kernel may reach another device: no remote copies, remote signals or barrier semaphores. Data moves between devices by JAX's collectives and lax.ppermute only.
A program may use at most 128 MiB of HBM per device.

v0:
```python
import jax
import jax.numpy as jnp
from jax import lax
from jax.sharding import PartitionSpec as P

KW = 2048
STEP = 64
MOMENTUM_RATE = 0.9
LEARN_RATE = 1.0


def per_device(
    tokens,
    cotangent,
    query_weight,
    slot_keys,
    values,
    momentum,
    page_ids,
    last_step,
    decay_rate,
    gate_weight,
    out_weight,
):
    tok_rows = tokens.shape[0]
    col_width = values.shape[1]
    key_width = slot_keys.shape[1]
    block_count, per_block = page_ids.shape
    block_rows = tok_rows // block_count
    pages_local = last_step.shape[0]
    page_slots = values.shape[0] // pages_local
    owners = lax.axis_size("tok")
    capacity = max(2, per_block * block_count // owners + 1)
    send_slots = owners * capacity
    listed_slots = per_block * page_slots
    elapsed = (STEP - last_step).astype(jnp.float32)
    factor = jnp.exp(-elapsed[:, None] * decay_rate[None, :])
    stored = values.reshape(pages_local, page_slots, col_width)
    decayed = (stored * factor[:, None, :]).astype(jnp.bfloat16)
    key_pages = slot_keys.reshape(pages_local, page_slots, key_width)
    token_piece = lax.all_gather(tokens, "col", axis=1, tiled=True)
    cotangent_piece = lax.all_gather(cotangent, "col", axis=1, tiled=True)
    query_sum = jnp.dot(token_piece, query_weight, preferred_element_type=jnp.float32)
    gate_logits = jnp.dot(token_piece, gate_weight, preferred_element_type=jnp.float32)
    grad_gated = jnp.einsum(
        "nd,cd->nc", cotangent_piece, out_weight, preferred_element_type=jnp.float32
    )
    requested = page_ids.reshape(-1)
    page_owner = requested // pages_local
    local_page = requested % pages_local
    request_count = requested.shape[0]
    positions = jnp.arange(request_count)
    same_owner = page_owner[:, None] == page_owner[None, :]
    slot_rank = jnp.sum(same_owner & (positions[None, :] < positions[:, None]), axis=1)
    send_slot = page_owner * capacity + slot_rank
    slot_match = send_slot[:, None] == jnp.arange(send_slots)[None, :]
    wanted = jnp.sum(jnp.where(slot_match, local_page[:, None] + 1, 0), axis=0) - 1
    wanted = wanted.reshape(owners, capacity)
    incoming = lax.all_to_all(wanted, "tok", split_axis=0, concat_axis=0, tiled=True)
    occupied = (incoming >= 0)[:, :, None, None]
    chosen = jnp.clip(incoming, 0, pages_local - 1)
    reply_keys = jnp.where(occupied, key_pages[chosen], jnp.zeros((), jnp.bfloat16))
    reply_values = jnp.where(occupied, decayed[chosen], jnp.zeros((), jnp.bfloat16))
    got_keys = lax.all_to_all(reply_keys, "tok", split_axis=0, concat_axis=0, tiled=True)
    got_values = lax.all_to_all(reply_values, "tok", split_axis=0, concat_axis=0, tiled=True)
    block_keys = got_keys.reshape(send_slots, page_slots, key_width)[send_slot]
    block_keys = block_keys.reshape(block_count, listed_slots, key_width)
    block_values = got_values.reshape(send_slots, page_slots, col_width)[send_slot]
    block_values = block_values.reshape(block_count, listed_slots, col_width)
    queries = query_sum.astype(jnp.bfloat16).reshape(block_count, block_rows, key_width)
    partial_scores = jnp.einsum(
        "bnk,bsk->bns", queries, block_keys, preferred_element_type=jnp.float32
    )
    score_scale = KW ** (-0.5)
    flat_scores = partial_scores.reshape(tok_rows, listed_slots)
    score_share = (
        lax.psum_scatter(flat_scores, "col", scatter_dimension=0, tiled=True) * score_scale
    )
    share_weights = jax.nn.softmax(score_share, axis=-1).astype(jnp.bfloat16)
    weights = lax.all_gather(share_weights, "col", axis=0, tiled=True).reshape(
        block_count, block_rows, listed_slots
    )
    memory = jnp.einsum("bns,bsd->bnd", weights, block_values, preferred_element_type=jnp.float32)
    memory = memory.reshape(tok_rows, col_width)
    activation = jax.nn.silu(gate_logits)
    gated_memory = (memory * activation).astype(jnp.bfloat16)
    out_terms = jnp.dot(gated_memory, out_weight, preferred_element_type=jnp.float32)
    layer_out = lax.psum_scatter(
        out_terms.astype(jnp.bfloat16), "col", scatter_dimension=1, tiled=True
    )
    grad_memory = (
        (grad_gated * activation).astype(jnp.bfloat16).reshape(block_count, block_rows, col_width)
    )
    slot_grads = jnp.einsum(
        "bns,bnd->bsd", weights, grad_memory, preferred_element_type=jnp.float32
    ).astype(jnp.bfloat16)
    outgoing = jnp.zeros((send_slots, page_slots, col_width), jnp.bfloat16)
    outgoing = outgoing.at[send_slot].set(slot_grads.reshape(request_count, page_slots, col_width))
    returned = lax.all_to_all(
        outgoing.reshape(owners, capacity, page_slots, col_width),
        "tok",
        split_axis=0,
        concat_axis=0,
        tiled=True,
    )
    page_match = incoming.reshape(1, send_slots) == jnp.arange(pages_local)[:, None]
    page_grad = jnp.dot(
        page_match.astype(jnp.bfloat16),
        returned.reshape(send_slots, page_slots * col_width),
        preferred_element_type=jnp.float32,
    )
    page_grad = page_grad.reshape(pages_local, page_slots, col_width)
    touched = jnp.any(page_match, axis=1)[:, None, None]
    moment = momentum.reshape(pages_local, page_slots, col_width)
    new_momentum = jnp.where(
        touched, MOMENTUM_RATE * moment + page_grad * factor[:, None, :], moment
    )
    new_values = jnp.where(touched, stored * factor[:, None, :] - LEARN_RATE * new_momentum, stored)
    return (layer_out, new_values.reshape(-1, col_width), new_momentum.reshape(-1, col_width))


def solution(mesh):
    in_specs = (
        P("tok", "col"),
        P("tok", "col"),
        P(None, "col"),
        P("tok", "col"),
        P("tok", "col"),
        P("tok", "col"),
        P("tok", None),
        P("tok"),
        P("col"),
        P(None, "col"),
        P("col", None),
    )
    out_specs = (P("tok", "col"), P("tok", "col"), P("tok", "col"))
    return jax.shard_map(
        per_device, mesh=mesh, in_specs=in_specs, out_specs=out_specs, check_vma=False
    )
```

profile of v0, /device:TPU:0, one launch (start us, length us, event | category | flops | bytes accessed | tf_op | source)
XLA Modules:
  0.0 1397.6 jit_solution(13270048119418362849)
XLA Ops:
  8.6 13.6 all_to_all.21
  22.6 7.5 gather_fusion
  30.1 14.0 %broadcast_select_fusion.1 = bf16[16,4,128,1024]{3,2,1,0:T(8,128)(2,1)} fusion(bf16[16,4,128,1024]{3,2,1,0:T(8,128)(2,1)} %bitcast.73, pred[16,4]{1,0:T(8,128)(4,1)S(1)} %copy.68), kind=kLoop, calls=%fused_computation.9 | loop fusion | flops 8388608 | bytes 33554496 | tf_op jit(solution)/shard_map/jit(_where)/select_n | solution.py:62
  50.9 46.9 %all-gather.3.cloned.1.call-done = bf16[768,2048]{1,0:T(8,128)(2,1)} async-done(((bf16[768,1024]{1,0:T(8,128)(2,1)}), bf16[768,2048]{1,0:T(8,128)(2,1)}) %all-gather.3.cloned.1.call-update) | async-done | bytes 3145744 | tf_op jit(solution)/shard_map/all_gather | solution.py:41
  97.7 6.6 convolution_convert_fusion.2
  104.3 241.5 %all-to-all-done.1 = bf16[16,4,128,1024]{3,2,1,0:T(8,128)(2,1)} async-done(((bf16[16,4,128,1024]{3,2,1,0:T(8,128)(2,1)}), bf16[16,4,128,1024]{3,2,1,0:T(8,128)(2,1)}, u32[]{:S(2)}, u32[]{:S(2)}) %all-to-all-start.1) | async-done | bytes 16777248 | tf_op jit(solution)/shard_map/all_to_all | solution.py:64
  345.8 12.1 gather_fusion.1
  357.9 9.6 fusion.15
  367.6 8.2 fusion.17
  375.8 7.7 multiply_convert_fusion
  383.5 75.9 %reduce-scatter.3.cloned.1.call-done = f32[384,512]{1,0:T(8,128)} async-done(((f32[768,512]{1,0:T(8,128)}), f32[384,512]{1,0:T(8,128)}) %reduce-scatter.3.cloned.1.call-update) | async-done | bytes 786448 | tf_op jit(solution)/shard_map/reduce_scatter | solution.py:77
  463.5 24.0 %all_gather.10 = bf16[768,512]{1,0:T(8,128)(2,1)S(1)} all-gather(bf16[384,512]{1,0:T(8,128)(2,1)S(1)} %divide_convert_fusion), channel_id=1, replica_groups=mesh['tok'=16,'col'=2] {'col'}, dimensions={0}, use_global_device_ids=true | all-gather | bytes 1179648 | tf_op jit(solution)/shard_map/all_gather | solution.py:80
  487.5 6.4 convolution_convert_fusion
  499.9 31.7 %scatter_fusion = bf16[64,128,1024]{2,1,0:T(8,128)(2,1)} fusion(bf16[64,128,1024]{2,1,0:T(8,128)(2,1)} %broadcast_in_dim.69, s32[48]{0:T(128)S(1)} %fusion.14, bf16[48,128,1024]{2,1,0:T(8,128)(2,1)} %bitcast.75), kind=kCustom, calls=%fused_computation.4 | custom fusion | bytes 37748928 | tf_op jit(solution)/shard_map/scatter | solution.py:98
  531.6 6.1 all-to-all-start.3
  539.2 295.1 %all-to-all-done.3 = bf16[16,4,128,1024]{3,2,1,0:T(8,128)(2,1)} async-done(((bf16[16,4,128,1024]{3,2,1,0:T(8,128)(2,1)}), bf16[16,4,128,1024]{3,2,1,0:T(8,128)(2,1)}, u32[]{:S(2)}, u32[]{:S(2)}) %all-to-all-start.3) | async-done | bytes 16777248 | tf_op jit(solution)/shard_map/all_to_all | solution.py:99
  834.3 36.8 %subtract_select_fusion = (f32[8,128,1024]{2,0,1:T(8,128)}, bf16[8,128,1024]{2,0,1:T(8,128)(2,1)S(1)}, f32[8,128,1024]{2,0,1:T(8,128)}) fusion(f32[8,128,1024]{2,1,0:T(8,128)} %bitcast.80, f32[8,1024]{1,0:T(8,128)S(1)} %multiply_exponential_fusion, pred[8]{0:T(512)(128)(4,1)S(1)} %fusion.10, s32[64]{0:T(128)S(1)} %eq.49, f32[8,128,1024]{2,1,0:T(8,128)} %bitcast.81, ...), kind=kOutput, calls=%fused_computation.11 | convolution fusion | flops 142606848 | bytes 35684616 | tf_op jit(solution)/shard_map/dot_general | solution.py:107
  872.3 7.5 gather_fusion.2
  879.7 8.3 broadcast_select_fusion
  888.0 431.9 %all_to_all.22 = bf16[16,4,128,1024]{3,2,1,0:T(8,128)(2,1)} all-to-all(bf16[16,4,128,1024]{3,2,1,0:T(8,128)(2,1)S(1)} %broadcast_select_fusion), channel_id=1, replica_groups=mesh['tok'=16,'col'=2] {'tok'}, dimensions={0} | all-to-all | bytes 33554432 | tf_op jit(solution)/shard_map/all_to_all | solution.py:65
  1319.9 12.1 gather_fusion.3
  1332.0 7.0 fusion.16
  1346.1 6.8 copy.78
  1357.3 33.3 %reduce-scatter.5.cloned.1.call-done = bf16[768,1024]{1,0:T(8,128)(2,1)} async-done(((bf16[768,2048]{1,0:T(8,128)(2,1)}), bf16[768,1024]{1,0:T(8,128)(2,1)}) %reduce-scatter.5.cloned.1.call-update) | async-done | bytes 1572880 | tf_op jit(solution)/shard_map/reduce_scatter | solution.py:88
  (56 shorter events, 32.7 us)
Async XLA Ops:
  7.2 15.4 %copy-start = (bf16[1024,1024]{1,0:T(8,128)(2,1)S(1)}, bf16[1024,1024]{1,0:T(8,128)(2,1)}, u32[]{:S(2)}) copy-start(bf16[1024,1024]{1,0:T(8,128)(2,1)} %param.14) | copy-start | bytes 6291460
  44.0 301.7 %all-to-all-start.1 = ((bf16[16,4,128,1024]{3,2,1,0:T(8,128)(2,1)}), bf16[16,4,128,1024]{3,2,1,0:T(8,128)(2,1)}, u32[]{:S(2)}, u32[]{:S(2)}) async-start(bf16[16,4,128,1024]{3,2,1,0:T(8,128)(2,1)} %broadcast_select_fusion.1), calls=%async_computation.1 | async-start | bytes 33554432 | tf_op jit(solution)/shard_map/all_to_all | solution.py:64
  49.2 48.5 %all-gather.3.cloned.1.call-start = ((), (), s32[]{:S(2)}) async-start(), calls=%async_computation.6 | async-start | bytes 4718592 | tf_op jit(solution)/shard_map/all_gather | solution.py:41
  49.9 325.9 %all-gather.5.cloned.1.call-start = ((), (), s32[]{:S(2)}) async-start(), calls=%async_computation.9 | async-start | bytes 4718592 | tf_op jit(solution)/shard_map/all_gather | solution.py:42
  50.7 408.7 %reduce-scatter.3.cloned.1.call-start = ((), (), s32[]{:S(2)}) async-start(), calls=%async_computation.7 | async-start | bytes 2359296 | tf_op jit(solution)/shard_map/reduce_scatter | solution.py:77
  531.6 6.1 copy-start.6
  531.6 6.2 copy-start.4
  531.6 302.7 %all-to-all-start.3 = ((bf16[16,4,128,1024]{3,2,1,0:T(8,128)(2,1)}), bf16[16,4,128,1024]{3,2,1,0:T(8,128)(2,1)}, u32[]{:S(2)}, u32[]{:S(2)}) async-start(bf16[16,4,128,1024]{3,2,1,0:T(8,128)(2,1)} %bitcast.70), calls=%async_computation.5 | async-start | bytes 33554432 | tf_op jit(solution)/shard_map/all_to_all | solution.py:99
  537.7 853.0 %reduce-scatter.5.cloned.1.call-start = ((), (), s32[]{:S(2)}) async-start(), calls=%async_computation.8 | async-start | bytes 4718592 | tf_op jit(solution)/shard_map/reduce_scatter | solution.py:88
  1332.0 7.0 copy-start.3
  1339.1 2.2 copy-start.5
  1346.1 6.8 copy-start.2
  1352.9 37.8 %copy-start.1 = (bf16[1024,1024]{1,0:T(8,128)(2,1)S(1)}, bf16[1024,1024]{1,0:T(8,128)(2,1)}, u32[]{:S(2)}) copy-start(bf16[1024,1024]{1,0:T(8,128)(2,1)} %param.14) | copy-start | bytes 6291460
Sparse Core Ops, SparseCore 0:
  51.6 46.1 all-gather.2
  99.3 44.8 all-gather.4
  367.7 91.6 reduce-scatter.2
  1346.2 44.3 reduce-scatter.4
where the time goes:
time: 1410 us; the launch traced here: 1400 us
  waiting for transfers between devices  694 us (49%)
  blocking collectives  469 us (33%)
  local copies, waits for them, and re-layouts  92.6 us (7%)
  matrix products  87.2 us (6%)
  other arithmetic  28.6 us (2%)
  between operations  14.3 us (1%)
    all_to_all x1, blocking collectives, per_device(): lax.all_to_all(reply_values, 'tok', split_axis=0, concat_axis=0, tiled=True)  432 us
    all_to_all x1, waiting for transfers between devices, per_device(): lax.all_to_all(outgoing.reshape(owners, capacity, page_slots, col_width),...  295 us
    all_to_all x1, waiting for transfers between devices, per_device(): lax.all_to_all(reply_keys, 'tok', split_axis=0, concat_axis=0, tiled=True)  241 us
    reduce_scatter x1, waiting for transfers between devices, per_device(): lax.psum_scatter(flat_scores, 'col', scatter_dimension=0, tiled=True)  75.9 us
    all_gather x1, waiting for transfers between devices, per_device(): token_piece = lax.all_gather(tokens, 'col', axis=1, tiled=True)  46.9 us
    dot_general x1, matrix products, per_device(): jnp.dot(page_match.astype(jnp.bfloat16), returned.reshape(send_slots, pag...  36.8 us
    reduce_scatter x1, waiting for transfers between devices, per_device(): lax.psum_scatter(out_terms.astype(jnp.bfloat16), 'col', scatter_dimension...  33.3 us
    scatter x1, local copies, waits for them, and re-layouts, per_device(): outgoing.at[send_slot]  31.7 us
  transfers between devices with their start and end apart: 6, of which 5 were waited for; matrix products, arithmetic and copies ran while one was open for 4% of the time, Pallas kernels for 0%

commit v1 on v0

--- a/solution.py
+++ b/solution.py
@@ -7,6 +7,11 @@
 STEP = 64
 MOMENTUM_RATE = 0.9
 LEARN_RATE = 1.0
+_treat_waves = lambda my_tile, x_part, axis_name: jnp.split(
+    lax.all_gather(jnp.concatenate([my_tile, x_part], axis=0), axis_name, tiled=True, axis=1),
+    [my_tile.shape[0]],
+    axis=0,
+)
 
 
 def per_device(
@@ -38,8 +43,7 @@
     stored = values.reshape(pages_local, page_slots, col_width)
     decayed = (stored * factor[:, None, :]).astype(jnp.bfloat16)
     key_pages = slot_keys.reshape(pages_local, page_slots, key_width)
-    token_piece = lax.all_gather(tokens, "col", axis=1, tiled=True)
-    cotangent_piece = lax.all_gather(cotangent, "col", axis=1, tiled=True)
+    token_piece, cotangent_piece = _treat_waves(tokens, cotangent, "col")
     query_sum = jnp.dot(token_piece, query_weight, preferred_element_type=jnp.float32)
     gate_logits = jnp.dot(token_piece, gate_weight, preferred_element_type=jnp.float32)
     grad_gated = jnp.einsum(

time: 1410 us -> 1400 us (level)
    all_to_all x1, waiting for transfers between devices: 241 us -> 205 us  [per_device(): lax.all_to_all(reply_keys, 'tok', split_axis=0, concat_axis=0, tiled=True)]
    all_gather x2 -> x1, waiting for transfers between devices: 46.9 us -> 81.2 us  [lax.all_gather(jnp.concatenate([my_tile, x_part], axis=0), axis_name, til...]
  transfers between devices with their start and end apart: 6 -> 5, of which waited for: 5 -> 5; matrix products, arithmetic and copies ran while one was open for 4% -> 2% of each run, Pallas kernels for 0% -> 0%
where the time goes in v1:
time: 1400 us
  waiting for transfers between devices  692 us (49%)
  blocking collectives  457 us (33%)
  local copies, waits for them, and re-layouts  94.5 us (7%)
  matrix products  94.2 us (7%)
  other arithmetic  31.7 us (2%)
  between operations  14.2 us (1%)
    all_to_all x1, blocking collectives, per_device(): lax.all_to_all(reply_values, 'tok', split_axis=0, concat_axis=0, tiled=True)  432 us
    all_to_all x1, waiting for transfers between devices, per_device(): lax.all_to_all(outgoing.reshape(owners, capacity, page_slots, col_width),...  295 us
    all_to_all x1, waiting for transfers between devices, per_device(): lax.all_to_all(reply_keys, 'tok', split_axis=0, concat_axis=0, tiled=True)  205 us
    all_gather x1, waiting for transfers between devices, lax.all_gather(jnp.concatenate([my_tile, x_part], axis=0), axis_name, til...  81.2 us
    reduce_scatter x1, waiting for transfers between devices, per_device(): lax.psum_scatter(flat_scores, 'col', scatter_dimension=0, tiled=True)  78.1 us
    dot_general x1, matrix products, per_device(): jnp.dot(page_match.astype(jnp.bfloat16), returned.reshape(send_slots, pag...  47.7 us
    reduce_scatter x1, waiting for transfers between devices, per_device(): lax.psum_scatter(out_terms.astype(jnp.bfloat16), 'col', scatter_dimension...  33.3 us
    scatter x1, local copies, waits for them, and re-layouts, per_device(): outgoing.at[send_slot]  31.7 us
  transfers between devices with their start and end apart: 5, of which 5 were waited for; matrix products, arithmetic and copies ran while one was open for 2% of the time, Pallas kernels for 0%

profile of v1, /device:TPU:0, one launch (start us, length us, event | category | flops | bytes accessed | tf_op | source)
XLA Modules:
  0.0 1395.8 jit_solution(2636985975134296763)
XLA Ops:
  8.6 13.6 all_to_all.21
  22.6 7.5 gather_fusion
  30.1 14.0 %broadcast_select_fusion.1 = bf16[16,4,128,1024]{3,2,1,0:T(8,128)(2,1)} fusion(bf16[16,4,128,1024]{3,2,1,0:T(8,128)(2,1)} %bitcast.70, pred[16,4]{1,0:T(8,128)(4,1)S(1)} %copy.68), kind=kLoop, calls=%fused_computation.9 | loop fusion | flops 8388608 | bytes 33554496 | tf_op jit(solution)/shard_map/jit(_where)/select_n | solution.py:66
  53.3 81.2 %all-gather.2.cloned.1.call-done = bf16[1536,2048]{1,0:T(8,128)(2,1)} async-done(((bf16[1536,1024]{1,0:T(8,128)(2,1)}), bf16[1536,2048]{1,0:T(8,128)(2,1)}) %all-gather.2.cloned.1.call-update) | async-done | bytes 6291472 | tf_op jit(solution)/shard_map/all_gather | solution.py:11
  134.6 6.6 fusion.17
  141.1 204.8 %all-to-all-done.1 = bf16[16,4,128,1024]{3,2,1,0:T(8,128)(2,1)} async-done(((bf16[16,4,128,1024]{3,2,1,0:T(8,128)(2,1)}), bf16[16,4,128,1024]{3,2,1,0:T(8,128)(2,1)}, u32[]{:S(2)}, u32[]{:S(2)}) %all-to-all-start.1) | async-done | bytes 16777248 | tf_op jit(solution)/shard_map/all_to_all | solution.py:68
  345.9 12.1 gather_fusion.1
  358.0 9.6 fusion.28
  367.7 6.7 divide_multiply_fusion
  381.5 78.1 %reduce-scatter.3.cloned.1.call-done = f32[384,512]{1,0:T(8,128)} async-done(((f32[768,512]{1,0:T(8,128)}), f32[384,512]{1,0:T(8,128)}) %reduce-scatter.3.cloned.1.call-update) | async-done | bytes 786448 | tf_op jit(solution)/shard_map/reduce_scatter | solution.py:81
  463.6 11.4 all_gather.7
  475.0 6.4 convolution_convert_fusion
  481.4 6.0 broadcast_in_dim.69
  487.4 31.7 %scatter_fusion = bf16[64,128,1024]{2,1,0:T(8,128)(2,1)} fusion(bf16[64,128,1024]{2,1,0:T(8,128)(2,1)} %broadcast_in_dim.69, s32[48]{0:T(128)S(1)} %fusion.27, bf16[48,128,1024]{2,1,0:T(8,128)(2,1)} %bitcast.72), kind=kCustom, calls=%fused_computation.4 | custom fusion | bytes 37748928 | tf_op jit(solution)/shard_map/scatter | solution.py:102
  519.1 6.0 all-to-all-start.3
  526.7 295.1 %all-to-all-done.3 = bf16[16,4,128,1024]{3,2,1,0:T(8,128)(2,1)} async-done(((bf16[16,4,128,1024]{3,2,1,0:T(8,128)(2,1)}), bf16[16,4,128,1024]{3,2,1,0:T(8,128)(2,1)}, u32[]{:S(2)}, u32[]{:S(2)}) %all-to-all-start.3) | async-done | bytes 16777248 | tf_op jit(solution)/shard_map/all_to_all | solution.py:103
  821.8 47.7 %subtract_select_fusion = (f32[8,128,1024]{2,0,1:T(8,128)}, bf16[8,128,1024]{2,0,1:T(8,128)(2,1)S(1)}, f32[8,128,1024]{2,0,1:T(8,128)}) fusion(f32[8,128,1024]{2,1,0:T(8,128)} %bitcast.77, f32[8,1024]{1,0:T(8,128)S(1)} %multiply_exponential_fusion, pred[8]{0:T(512)(128)(4,1)S(1)} %fusion.23, s32[64]{0:T(128)S(1)} %eq.49, f32[8,128,1024]{2,1,0:T(8,128)} %bitcast.78, ...), kind=kOutput, calls=%fused_computation.11 | convolution fusion | flops 142606848 | bytes 35684616 | tf_op jit(solution)/shard_map/dot_general | solution.py:111
  870.6 7.5 gather_fusion.2
  878.1 8.3 broadcast_select_fusion
  886.4 431.9 %all_to_all.22 = bf16[16,4,128,1024]{3,2,1,0:T(8,128)(2,1)} all-to-all(bf16[16,4,128,1024]{3,2,1,0:T(8,128)(2,1)S(1)} %broadcast_select_fusion), channel_id=1, replica_groups=mesh['tok'=16,'col'=2] {'tok'}, dimensions={0} | all-to-all | bytes 33554432 | tf_op jit(solution)/shard_map/all_to_all | solution.py:69
  1318.3 12.1 gather_fusion.3
  1330.4 7.0 fusion.29
  1344.5 6.8 copy.78
  1355.7 33.3 %reduce-scatter.5.cloned.1.call-done = bf16[768,1024]{1,0:T(8,128)(2,1)} async-done(((bf16[768,2048]{1,0:T(8,128)(2,1)}), bf16[768,1024]{1,0:T(8,128)(2,1)}) %reduce-scatter.5.cloned.1.call-update) | async-done | bytes 1572880 | tf_op jit(solution)/shard_map/reduce_scatter | solution.py:92
  (60 shorter events, 36.3 us)
Async XLA Ops:
  7.2 15.4 %copy-start = (bf16[1024,1024]{1,0:T(8,128)(2,1)S(1)}, bf16[1024,1024]{1,0:T(8,128)(2,1)}, u32[]{:S(2)}) copy-start(bf16[1024,1024]{1,0:T(8,128)(2,1)} %param.14) | copy-start | bytes 6291460
  44.0 5.3 copy-start.5
  44.0 301.9 %all-to-all-start.1 = ((bf16[16,4,128,1024]{3,2,1,0:T(8,128)(2,1)}), bf16[16,4,128,1024]{3,2,1,0:T(8,128)(2,1)}, u32[]{:S(2)}, u32[]{:S(2)}) async-start(bf16[16,4,128,1024]{3,2,1,0:T(8,128)(2,1)} %broadcast_select_fusion.1), calls=%async_computation.1 | async-start | bytes 33554432 | tf_op jit(solution)/shard_map/all_to_all | solution.py:68
  49.3 85.2 %all-gather.2.cloned.1.call-start = ((), (), s32[]{:S(2)}) async-start(), calls=%async_computation.6 | async-start | bytes 9437184 | tf_op jit(solution)/shard_map/all_gather | solution.py:11
  52.8 406.8 %reduce-scatter.3.cloned.1.call-start = ((), (), s32[]{:S(2)}) async-start(), calls=%async_computation.7 | async-start | bytes 2359296 | tf_op jit(solution)/shard_map/reduce_scatter | solution.py:81
  367.7 8.4 copy-start.7
  374.5 1.7 copy-start.3
  519.1 6.1 copy-start.9
  519.1 6.1 copy-start.6
  519.1 302.7 %all-to-all-start.3 = ((bf16[16,4,128,1024]{3,2,1,0:T(8,128)(2,1)}), bf16[16,4,128,1024]{3,2,1,0:T(8,128)(2,1)}, u32[]{:S(2)}, u32[]{:S(2)}) async-start(bf16[16,4,128,1024]{3,2,1,0:T(8,128)(2,1)} %bitcast.67), calls=%async_computation.5 | async-start | bytes 33554432 | tf_op jit(solution)/shard_map/all_to_all | solution.py:103
  525.2 863.8 %reduce-scatter.5.cloned.1.call-start = ((), (), s32[]{:S(2)}) async-start(), calls=%async_computation.8 | async-start | bytes 4718592 | tf_op jit(solution)/shard_map/reduce_scatter | solution.py:92
  1330.4 7.0 copy-start.4
  1337.4 2.2 copy-start.8
  1344.5 6.8 copy-start.2
  1351.3 37.7 %copy-start.1 = (bf16[1024,1024]{1,0:T(8,128)(2,1)S(1)}, bf16[1024,1024]{1,0:T(8,128)(2,1)}, u32[]{:S(2)}) copy-start(bf16[1024,1024]{1,0:T(8,128)(2,1)} %param.14) | copy-start | bytes 6291460
Sparse Core Ops, SparseCore 0:
  52.9 81.5 all-gather.1
  367.8 91.7 reduce-scatter.2
  1344.6 44.3 reduce-scatter.4
